TPU v7x, 512 devices: a whole 4x4x16 slice. The times are simulated.
512 devices in a mesh: segment: 8 (over x, core), dp: 64 (over y, z).
Axes of the slice: x: 4, y: 4, z: 16, core: 2. Of those that a mesh axis runs over, the one named last changes fastest.
Arguments:
- hidden: bfloat16 [8, 8192, 8192], P('segment', 'dp'), may hold values from -6 to 6
- store_a: bfloat16 [8, 32, 64, 8192], P('segment', None, None, 'dp'), may hold values from -0.0625 to 0.0625
- store_b: bfloat16 [8, 32, 64, 8192], P('segment', None, None, 'dp'), may hold values from -0.75 to 0.75
- request_start: int32 [8, 32], P('segment'), may hold values from 0 to 8128, as said below
- request_adapter: int32 [8, 32], P('segment'), may hold values from 0 to 31
Outputs:
- updated: bfloat16 [8, 8192, 8192], P('segment', 'dp')
Inputs may be any that keep to these rules, and one draw needn't show every extreme that they name: `request_start`: in each group the starts rise strictly from 0, are multiples of 64, and the last is 8128.
All inputs are finite; a program needn't handle non-finite values.
Results may differ from a plain program's by a relative error of at most 0.006.
Values may be sent and summed in bfloat16 or wider, within the bound.
No kernel may reach another device: no remote copies, remote signals or barrier semaphores. Data moves between devices by JAX's collectives and lax.ppermute only.
A program may use at most 64 MiB of HBM per device.

v0:
```python
import jax
import jax.numpy as jnp
from jax import lax
from jax.sharding import PartitionSpec as P

BLOCK = 64
STEPS = 2
EPS = 1e-05
ADAPTER_SCALE = 0.5


def from_behind(block, axis, distance):
    devices = range(lax.axis_size(axis))
    route = [((i - distance) % len(devices), i) for i in devices]
    return lax.ppermute(block, axis, route)


def block_adapters(starts, adapters, total_rows):
    blocks = total_rows // BLOCK
    block_start = jnp.arange(blocks, dtype=jnp.int32) * BLOCK
    request = jnp.sum((starts[None, :] <= block_start[:, None]).astype(jnp.int32), axis=1) - 1
    labels = jnp.arange(adapters.shape[0], dtype=jnp.int32)
    picked = jnp.where(request[:, None] == labels[None, :], adapters[None, :], 0)
    return jnp.sum(picked, axis=1)


def apply_layer(state, starts, adapters, slice_a, slice_b):
    value_rows = state.astype(jnp.float32)
    meansq = jnp.mean(value_rows * value_rows, axis=-1, keepdims=True)
    normed = (value_rows * lax.rsqrt(meansq + EPS)).astype(jnp.bfloat16)
    rank_width = slice_a.shape[1]
    columns = lax.all_to_all(normed, "dp", split_axis=1, concat_axis=0, tiled=True)
    total_rows, width = columns.shape
    blocks = total_rows // BLOCK
    chosen = block_adapters(starts, adapters, total_rows)
    down = jnp.take(slice_a, chosen, axis=0)
    grouped = columns.reshape(blocks, BLOCK, width)
    partial_rank = jnp.einsum("bic,brc->bir", grouped, down, preferred_element_type=jnp.float32)
    partial_rank = partial_rank.reshape(total_rows, rank_width)
    rank = lax.psum(partial_rank, "dp").astype(jnp.bfloat16)
    upper = jnp.take(slice_b, chosen, axis=0)
    adapter_update = jnp.einsum(
        "bir,brc->bic",
        rank.reshape(blocks, BLOCK, rank_width),
        upper,
        preferred_element_type=jnp.float32,
    )
    adapter_update = adapter_update.reshape(total_rows, width).astype(jnp.bfloat16)
    returned_rows = lax.all_to_all(adapter_update, "dp", split_axis=0, concat_axis=1, tiled=True)
    return (value_rows + ADAPTER_SCALE * returned_rows.astype(jnp.float32)).astype(jnp.bfloat16)


def shards(hidden, store_a, store_b, request_start, request_adapter):
    state = hidden[0]
    starts = request_start[0]
    adapters = request_adapter[0]
    slice_a = store_a[0]
    slice_b = store_b[0]
    for step in range(STEPS):
        if step > 0:
            state = from_behind(state, "segment", 1)
            starts, adapters = from_behind((starts, adapters), "segment", 1)
        state = apply_layer(state, starts, adapters, slice_a, slice_b)
    state = from_behind(state, "segment", 1 - STEPS)
    return state[None]


def solution(mesh):
    return jax.shard_map(
        shards,
        mesh=mesh,
        in_specs=(
            P("segment", "dp", None),
            P("segment", None, None, "dp"),
            P("segment", None, None, "dp"),
            P("segment", None),
            P("segment", None),
        ),
        out_specs=P("segment", "dp", None),
        check_vma=False,
    )
```

profile of v0, /device:TPU:45, one launch (start us, length us, event | category | flops | bytes accessed | tf_op | source)
XLA Modules:
  0.0 1126.6 jit_solution(4705812348207641893)
XLA Ops:
  0.0 0.0 copy-start
  0.0 0.0 copy-start.2
  0.0 2.2 convert_bitcast_fusion
  2.2 0.1 copy-done.2
  2.3 0.5 fusion.2
  2.8 0.7 copy.17
  3.5 3.8 fusion.7
  7.3 0.0 copy-start.3
  7.3 0.0 copy-start.4
  7.3 18.0 %all-to-all-start = ((bf16[128,64,128]{2,0,1:T(8,128)(2,1)}), bf16[128,64,128]{2,0,1:T(8,128)(2,1)}, u32[]{:S(2)}, u32[]{:S(2)}) async-start(bf16[128,64,128]{2,0,1:T(8,128)(2,1)} %fusion.7), calls=%async_computation | async-start | bytes 4194304 | tf_op jit(solution)/shard_map/all_to_all | solution.py:32
  25.3 0.0 copy-done.3
  25.4 2.0 collective-permute-start.1
  27.4 0.7 collective-permute-done.1
  28.1 0.1 convert_reduce_fusion
  28.2 0.0 copy-done.4
  28.2 0.1 select_reduce_fusion.1
  28.3 0.0 copy-done
  28.3 0.0 copy-start.1
  28.4 2.2 gather_fusion
  30.6 0.0 copy-done.1
  30.6 2.1 gather_fusion.1
  32.7 89.3 %all-to-all-done = bf16[128,64,128]{2,0,1:T(8,128)(2,1)} async-done(((bf16[128,64,128]{2,0,1:T(8,128)(2,1)}), bf16[128,64,128]{2,0,1:T(8,128)(2,1)}, u32[]{:S(2)}, u32[]{:S(2)}) %all-to-all-start) | async-done | bytes 2097184 | tf_op jit(solution)/shard_map/all_to_all | solution.py:32
  122.1 5.4 fusion.15
  127.5 248.0 %all-reduce.2 = bf16[8192,64]{1,0:T(8,128)(2,1)} all-reduce(f32[8192,64]{1,0:T(8,128)} %bitcast.57), channel_id=1, replica_groups=mesh['segment'=8,'dp'=64] {'dp'}, use_global_device_ids=true, to_apply=%region_3.5 | all-reduce | flops 524288 | bytes 3145728 | tf_op jit(solution)/shard_map/psum | solution.py:40
  375.5 3.0 fusion.21
  378.5 82.6 %all_to_all.49 = bf16[64,128,128]{2,1,0:T(8,128)(2,1)S(1)} all-to-all(bf16[64,128,128]{2,1,0:T(8,128)(2,1)S(1)} %bitcast.61), channel_id=1, replica_groups=mesh['segment'=8,'dp'=64] {'dp'}, dimensions={0} | all-to-all | bytes 4194304 | tf_op jit(solution)/shard_map/all_to_all | solution.py:49
  461.1 0.7 fusion.3
  461.7 84.9 %collective-permute-start = (bf16[128,8192]{1,0:T(8,128)(2,1)S(1)}, bf16[128,8192]{1,0:T(8,128)(2,1)S(1)}, u32[]{:S(2)}, u32[]{:S(2)}) collective-permute-start(bf16[128,8192]{1,0:T(8,128)(2,1)S(1)} %fusion.3), channel_id=1, source_target_pairs={{448,0},{0,64},{64,128},{128,192},{192,256},{256,320},{320,384},{3... | collective-permute-start | bytes 6291464 | tf_op jit(solution)/shard_map/ppermute | solution.py:15
  546.6 23.0 %collective-permute-done = bf16[128,8192]{1,0:T(8,128)(2,1)S(1)} collective-permute-done((bf16[128,8192]{1,0:T(8,128)(2,1)S(1)}, bf16[128,8192]{1,0:T(8,128)(2,1)S(1)}, u32[]{:S(2)}, u32[]{:S(2)}) %collective-permute-start) | collective-permute-done | bytes 2097184 | tf_op jit(solution)/shard_map/ppermute | solution.py:15
  569.6 0.5 fusion.4
  570.1 2.0 copy_bitcast_fusion
  572.0 7.3 all-to-all-start.2
  579.3 3.1 collective-permute-start.2
  582.4 0.7 collective-permute-done.2
  583.1 0.1 select_reduce_fusion
  583.2 2.2 gather_fusion.2
  585.4 2.1 gather_fusion.3
  587.6 87.6 %all-to-all-done.2 = bf16[128,64,128]{2,0,1:T(8,128)(2,1)} async-done(((bf16[128,64,128]{2,0,1:T(8,128)(2,1)}), bf16[128,64,128]{2,0,1:T(8,128)(2,1)}, u32[]{:S(2)}, u32[]{:S(2)}) %all-to-all-start.2) | async-done | bytes 2097184 | tf_op jit(solution)/shard_map/all_to_all | solution.py:32
  675.2 5.4 fusion.11
  680.7 246.4 %all-reduce.3 = bf16[8192,64]{1,0:T(8,128)(2,1)} all-reduce(f32[8192,64]{1,0:T(8,128)} %bitcast.58), channel_id=1, replica_groups=mesh['segment'=8,'dp'=64] {'dp'}, use_global_device_ids=true, to_apply=%region_7.9 | all-reduce | flops 524288 | bytes 3145728 | tf_op jit(solution)/shard_map/psum | solution.py:40
  927.0 3.0 fusion.24
  930.0 83.2 %all_to_all.50 = bf16[64,128,128]{2,1,0:T(8,128)(2,1)S(1)} all-to-all(bf16[64,128,128]{2,1,0:T(8,128)(2,1)S(1)} %bitcast.62), channel_id=1, replica_groups=mesh['segment'=8,'dp'=64] {'dp'}, dimensions={0} | all-to-all | bytes 4194304 | tf_op jit(solution)/shard_map/all_to_all | solution.py:49
  1013.2 0.7 fusion.6
  1013.9 84.6 %collective-permute-start.3 = (bf16[128,8192]{1,0:T(8,128)(2,1)S(1)}, bf16[128,8192]{1,0:T(8,128)(2,1)S(1)}, u32[]{:S(2)}, u32[]{:S(2)}) collective-permute-start(bf16[128,8192]{1,0:T(8,128)(2,1)S(1)} %fusion.6), channel_id=1, source_target_pairs={{64,0},{128,64},{192,128},{256,192},{320,256},{384,320},{448,384},... | collective-permute-start | bytes 6291464 | tf_op jit(solution)/shard_map/ppermute | solution.py:15
  1098.5 26.9 %collective-permute-done.3 = bf16[128,8192]{1,0:T(8,128)(2,1)S(1)} collective-permute-done((bf16[128,8192]{1,0:T(8,128)(2,1)S(1)}, bf16[128,8192]{1,0:T(8,128)(2,1)S(1)}, u32[]{:S(2)}, u32[]{:S(2)}) %collective-permute-start.3) | collective-permute-done | bytes 2097184 | tf_op jit(solution)/shard_map/ppermute | solution.py:15
  1125.3 1.3 copy.29
  (11 shorter events, 0.1 us)
Async XLA Ops:
  0.0 28.3 %copy-start = (bf16[1,32,64,128]{3,2,1,0:T(8,128)(2,1)S(1)}, bf16[1,32,64,128]{3,2,1,0:T(8,128)(2,1)}, u32[]{:S(2)}) copy-start(bf16[1,32,64,128]{3,2,1,0:T(8,128)(2,1)} %param.8) | copy-start | bytes 1572868
  0.0 2.3 copy-start.2
  7.3 18.1 %copy-start.3 = (s32[1,32]{1,0:T(1,128)S(1)}, s32[1,32]{1,0:T(1,128)}, u32[]{:S(2)}) copy-start(s32[1,32]{1,0:T(1,128)} %param.10) | copy-start | bytes 388
  7.3 20.9 %copy-start.4 = (s32[1,32]{1,0:T(1,128)S(1)}, s32[1,32]{1,0:T(1,128)}, u32[]{:S(2)}) copy-start(s32[1,32]{1,0:T(1,128)} %param.11) | copy-start | bytes 388
  7.3 114.8 %all-to-all-start = ((bf16[128,64,128]{2,0,1:T(8,128)(2,1)}), bf16[128,64,128]{2,0,1:T(8,128)(2,1)}, u32[]{:S(2)}, u32[]{:S(2)}) async-start(bf16[128,64,128]{2,0,1:T(8,128)(2,1)} %fusion.7), calls=%async_computation | async-start | bytes 4194304 | tf_op jit(solution)/shard_map/all_to_all | solution.py:32
  25.4 2.8 collective-permute-start.1
  28.3 2.2 copy-start.1
  461.7 107.9 %collective-permute-start = (bf16[128,8192]{1,0:T(8,128)(2,1)S(1)}, bf16[128,8192]{1,0:T(8,128)(2,1)S(1)}, u32[]{:S(2)}, u32[]{:S(2)}) collective-permute-start(bf16[128,8192]{1,0:T(8,128)(2,1)S(1)} %fusion.3), channel_id=1, source_target_pairs={{448,0},{0,64},{64,128},{128,192},{192,256},{256,320},{320,384},{3... | collective-permute-start | bytes 6291464 | tf_op jit(solution)/shard_map/ppermute | solution.py:15
  572.0 103.2 %all-to-all-start.2 = ((bf16[128,64,128]{2,0,1:T(8,128)(2,1)}), bf16[128,64,128]{2,0,1:T(8,128)(2,1)}, u32[]{:S(2)}, u32[]{:S(2)}) async-start(bf16[128,64,128]{2,0,1:T(8,128)(2,1)} %copy_bitcast_fusion), calls=%async_computation.2 | async-start | bytes 4194304 | tf_op jit(solution)/shard_map/all_to_all | solution.py:32
  579.3 3.8 collective-permute-start.2
  1013.9 111.4 %collective-permute-start.3 = (bf16[128,8192]{1,0:T(8,128)(2,1)S(1)}, bf16[128,8192]{1,0:T(8,128)(2,1)S(1)}, u32[]{:S(2)}, u32[]{:S(2)}) collective-permute-start(bf16[128,8192]{1,0:T(8,128)(2,1)S(1)} %fusion.6), channel_id=1, source_target_pairs={{64,0},{128,64},{192,128},{256,192},{320,256},{384,320},{448,384},... | collective-permute-start | bytes 6291464 | tf_op jit(solution)/shard_map/ppermute | solution.py:15
where the time goes:
time: 1130 us
  blocking collectives  660 us (58%)
  waiting for transfers between devices  228 us (20%)
  starting transfers between devices  200 us (18%)
  matrix products  16.9 us (1%)
    psum x2, blocking collectives, apply_layer(): rank = lax.psum(partial_rank, 'dp').astype(jnp.bfloat16)  494 us
    all_to_all x2, waiting for transfers between devices, apply_layer(): lax.all_to_all(normed, 'dp', split_axis=1, concat_axis=0, tiled=True)  177 us
    ppermute x4, starting transfers between devices, from_behind(): return lax.ppermute(block, axis, route)  175 us
    all_to_all x2, blocking collectives, apply_layer(): lax.all_to_all(adapter_update, 'dp', split_axis=0, concat_axis=1, tiled=T...  166 us
    ppermute x4, waiting for transfers between devices, from_behind(): return lax.ppermute(block, axis, route)  51.3 us
    all_to_all x2, starting transfers between devices, apply_layer(): lax.all_to_all(normed, 'dp', split_axis=1, concat_axis=0, tiled=True)  25.4 us
  transfers between devices with their start and end apart: 6, of which 6 were waited for; matrix products, arithmetic and copies ran while one was open for 1% of the time, Pallas kernels for 0%

commit v1 on v0

--- a/solution.py
+++ b/solution.py
@@ -29,7 +29,10 @@
     meansq = jnp.mean(value_rows * value_rows, axis=-1, keepdims=True)
     normed = (value_rows * lax.rsqrt(meansq + EPS)).astype(jnp.bfloat16)
     rank_width = slice_a.shape[1]
-    columns = lax.all_to_all(normed, "dp", split_axis=1, concat_axis=0, tiled=True)
+    columns = jnp.concatenate(
+        lax.all_to_all(jnp.stack(jnp.split(normed, lax.axis_size("dp"), axis=1)), "dp", 0, 0),
+        axis=0,
+    )
     total_rows, width = columns.shape
     blocks = total_rows // BLOCK
     chosen = block_adapters(starts, adapters, total_rows)

time: 1130 us -> 1200 us (1.062)
  the two profiles are of different devices: /device:TPU:45 before, /device:TPU:1 now
where the time goes in v1:
time: 1200 us
  blocking collectives  668 us (56%)
  waiting for transfers between devices  219 us (18%)
  starting transfers between devices  200 us (17%)
  local copies, waits for them, and re-layouts  90 us (8%)
  matrix products  16.9 us (1%)
    psum x2, blocking collectives, apply_layer(): rank = lax.psum(partial_rank, 'dp').astype(jnp.bfloat16)  554 us
    ppermute x4, starting transfers between devices, from_behind(): return lax.ppermute(block, axis, route)  172 us
    all_to_all x2, waiting for transfers between devices, apply_layer(): lax.all_to_all(jnp.stack(jnp.split(normed, lax.axis_size('dp'), axis=1)),...  170 us
    all_to_all x2, blocking collectives, apply_layer(): lax.all_to_all(adapter_update, 'dp', split_axis=0, concat_axis=1, tiled=T...  114 us
    unnamed x137, local copies, waits for them, and re-layouts  80 us
    ppermute x4, waiting for transfers between devices, from_behind(): return lax.ppermute(block, axis, route)  48.4 us
    all_to_all x2, starting transfers between devices, apply_layer(): lax.all_to_all(jnp.stack(jnp.split(normed, lax.axis_size('dp'), axis=1)),...  28.6 us
  transfers between devices with their start and end apart: 6, of which 6 were waited for; matrix products, arithmetic and copies ran while one was open for 1% of the time, Pallas kernels for 0%

profile of v1, /device:TPU:1, one launch (start us, length us, event | category | flops | bytes accessed | tf_op | source)
XLA Modules:
  0.0 1199.3 jit_solution(10479302093871429923)
XLA Ops:
  0.0 2.2 fusion.3
  2.7 0.6 constant_dynamic-update-slice_fusion.63
  3.4 0.6 constant_dynamic-update-slice_fusion.62
  4.0 0.6 constant_dynamic-update-slice_fusion.61
  4.6 0.6 constant_dynamic-update-slice_fusion.60
  7.1 0.6 constant_dynamic-update-slice_fusion.56
  7.7 0.6 constant_dynamic-update-slice_fusion.55
  8.4 0.6 constant_dynamic-update-slice_fusion.54
  10.9 0.6 constant_dynamic-update-slice_fusion.50
  11.5 0.6 constant_dynamic-update-slice_fusion.49
  12.1 0.6 constant_dynamic-update-slice_fusion.48
  12.7 0.6 constant_dynamic-update-slice_fusion.47
  15.2 0.6 constant_dynamic-update-slice_fusion.43
  15.9 0.6 constant_dynamic-update-slice_fusion.42
  16.5 0.6 constant_dynamic-update-slice_fusion.41
  19.0 0.6 constant_dynamic-update-slice_fusion.37
  19.6 0.6 constant_dynamic-update-slice_fusion.36
  20.2 0.6 constant_dynamic-update-slice_fusion.35
  22.7 0.6 constant_dynamic-update-slice_fusion.31
  23.3 0.6 constant_dynamic-update-slice_fusion.30
  42.7 19.7 %all-to-all-start = ((bf16[64,128,128]{2,1,0:T(8,128)(2,1)}), bf16[64,128,128]{2,1,0:T(8,128)(2,1)}, u32[]{:S(2)}, u32[]{:S(2)}) async-start(bf16[64,128,128]{2,1,0:T(8,128)(2,1)} %constant_dynamic-update-slice_fusion), calls=%async_computation | async-start | bytes 4194304 | tf_op jit(solution)/shard_map/all_to_all | solution.py:33
  62.4 2.1 collective-permute-start.1
  64.5 0.7 collective-permute-done.1
  65.4 2.2 gather_fusion
  67.6 2.1 gather_fusion.1
  69.8 87.3 %all-to-all-done = bf16[64,128,128]{2,1,0:T(8,128)(2,1)} async-done(((bf16[64,128,128]{2,1,0:T(8,128)(2,1)}), bf16[64,128,128]{2,1,0:T(8,128)(2,1)}, u32[]{:S(2)}, u32[]{:S(2)}) %all-to-all-start) | async-done | bytes 2097184 | tf_op jit(solution)/shard_map/all_to_all | solution.py:33
  157.1 5.4 fusion.12
  162.5 275.2 %all-reduce.2 = bf16[8192,64]{1,0:T(8,128)(2,1)} all-reduce(f32[8192,64]{1,0:T(8,128)} %bitcast.550), channel_id=1, replica_groups=mesh['segment'=8,'dp'=64] {'dp'}, use_global_device_ids=true, to_apply=%region_3.5 | all-reduce | flops 524288 | bytes 3145728 | tf_op jit(solution)/shard_map/psum | solution.py:43
  437.7 3.0 fusion.18
  440.7 57.8 %all_to_all.30 = bf16[64,128,128]{2,1,0:T(8,128)(2,1)S(1)} all-to-all(bf16[64,128,128]{2,1,0:T(8,128)(2,1)S(1)} %bitcast.554), channel_id=1, replica_groups=mesh['segment'=8,'dp'=64] {'dp'}, dimensions={0} | all-to-all | bytes 4194304 | tf_op jit(solution)/shard_map/all_to_all | solution.py:52
  498.5 0.6 fusion.5
  499.2 83.1 %collective-permute-start = (bf16[128,8192]{1,0:T(8,128)(2,1)S(1)}, bf16[128,8192]{1,0:T(8,128)(2,1)S(1)}, u32[]{:S(2)}, u32[]{:S(2)}) collective-permute-start(bf16[128,8192]{1,0:T(8,128)(2,1)S(1)} %fusion.5), channel_id=1, source_target_pairs={{448,0},{0,64},{64,128},{128,192},{192,256},{256,320},{320,384},{3... | collective-permute-start | bytes 6291464 | tf_op jit(solution)/shard_map/ppermute | solution.py:15
  582.2 23.0 %collective-permute-done = bf16[128,8192]{1,0:T(8,128)(2,1)S(1)} collective-permute-done((bf16[128,8192]{1,0:T(8,128)(2,1)S(1)}, bf16[128,8192]{1,0:T(8,128)(2,1)S(1)}, u32[]{:S(2)}, u32[]{:S(2)}) %collective-permute-start) | collective-permute-done | bytes 2097184 | tf_op jit(solution)/shard_map/ppermute | solution.py:15
  606.2 0.6 constant_dynamic-update-slice_fusion.127
  646.2 8.9 all-to-all-start.2
  655.1 2.8 collective-permute-start.2
  657.9 1.0 collective-permute-done.2
  658.9 2.2 gather_fusion.2
  661.1 2.1 gather_fusion.3
  663.3 83.0 %all-to-all-done.2 = bf16[64,128,128]{2,1,0:T(8,128)(2,1)} async-done(((bf16[64,128,128]{2,1,0:T(8,128)(2,1)}), bf16[64,128,128]{2,1,0:T(8,128)(2,1)}, u32[]{:S(2)}, u32[]{:S(2)}) %all-to-all-start.2) | async-done | bytes 2097184 | tf_op jit(solution)/shard_map/all_to_all | solution.py:33
  746.3 5.4 fusion.8
  751.8 279.1 %all-reduce.3 = bf16[8192,64]{1,0:T(8,128)(2,1)} all-reduce(f32[8192,64]{1,0:T(8,128)} %bitcast.551), channel_id=1, replica_groups=mesh['segment'=8,'dp'=64] {'dp'}, use_global_device_ids=true, to_apply=%region_7.9 | all-reduce | flops 524288 | bytes 3145728 | tf_op jit(solution)/shard_map/psum | solution.py:43
  1030.9 3.0 fusion.21
  1033.9 55.8 %all_to_all.31 = bf16[64,128,128]{2,1,0:T(8,128)(2,1)S(1)} all-to-all(bf16[64,128,128]{2,1,0:T(8,128)(2,1)S(1)} %bitcast.555), channel_id=1, replica_groups=mesh['segment'=8,'dp'=64] {'dp'}, dimensions={0} | all-to-all | bytes 4194304 | tf_op jit(solution)/shard_map/all_to_all | solution.py:52
  1089.6 0.6 fusion.2
  1090.3 84.0 %collective-permute-start.3 = (bf16[128,8192]{1,0:T(8,128)(2,1)S(1)}, bf16[128,8192]{1,0:T(8,128)(2,1)S(1)}, u32[]{:S(2)}, u32[]{:S(2)}) collective-permute-start(bf16[128,8192]{1,0:T(8,128)(2,1)S(1)} %fusion.2), channel_id=1, source_target_pairs={{64,0},{128,64},{192,128},{256,192},{320,256},{384,320},{448,384},... | collective-permute-start | bytes 6291464 | tf_op jit(solution)/shard_map/ppermute | solution.py:15
  1174.3 23.8 %collective-permute-done.3 = bf16[128,8192]{1,0:T(8,128)(2,1)S(1)} collective-permute-done((bf16[128,8192]{1,0:T(8,128)(2,1)S(1)}, bf16[128,8192]{1,0:T(8,128)(2,1)S(1)}, u32[]{:S(2)}, u32[]{:S(2)}) %collective-permute-start.3) | collective-permute-done | bytes 2097184 | tf_op jit(solution)/shard_map/ppermute | solution.py:15
  1198.0 1.3 copy.145
  (135 shorter events, 69.2 us)
Async XLA Ops:
  0.0 65.4 %copy-start = (bf16[1,32,64,128]{3,2,1,0:T(8,128)(2,1)S(1)}, bf16[1,32,64,128]{3,2,1,0:T(8,128)(2,1)}, u32[]{:S(2)}) copy-start(bf16[1,32,64,128]{3,2,1,0:T(8,128)(2,1)} %param.8) | copy-start | bytes 1572868
  0.0 2.3 copy-start.2
  42.7 19.7 %copy-start.3 = (s32[1,32]{1,0:T(1,128)S(1)}, s32[1,32]{1,0:T(1,128)}, u32[]{:S(2)}) copy-start(s32[1,32]{1,0:T(1,128)} %param.10) | copy-start | bytes 388
  42.7 22.6 %copy-start.4 = (s32[1,32]{1,0:T(1,128)S(1)}, s32[1,32]{1,0:T(1,128)}, u32[]{:S(2)}) copy-start(s32[1,32]{1,0:T(1,128)} %param.11) | copy-start | bytes 388
  42.7 114.4 %all-to-all-start = ((bf16[64,128,128]{2,1,0:T(8,128)(2,1)}), bf16[64,128,128]{2,1,0:T(8,128)(2,1)}, u32[]{:S(2)}, u32[]{:S(2)}) async-start(bf16[64,128,128]{2,1,0:T(8,128)(2,1)} %constant_dynamic-update-slice_fusion), calls=%async_computation | async-start | bytes 4194304 | tf_op jit(solution)/shard_map/all_to_all | solution.py:33
  62.4 2.8 collective-permute-start.1
  65.4 2.2 copy-start.1
  499.2 106.0 %collective-permute-start = (bf16[128,8192]{1,0:T(8,128)(2,1)S(1)}, bf16[128,8192]{1,0:T(8,128)(2,1)S(1)}, u32[]{:S(2)}, u32[]{:S(2)}) collective-permute-start(bf16[128,8192]{1,0:T(8,128)(2,1)S(1)} %fusion.5), channel_id=1, source_target_pairs={{448,0},{0,64},{64,128},{128,192},{192,256},{256,320},{320,384},{3... | collective-permute-start | bytes 6291464 | tf_op jit(solution)/shard_map/ppermute | solution.py:15
  646.2 100.2 %all-to-all-start.2 = ((bf16[64,128,128]{2,1,0:T(8,128)(2,1)}), bf16[64,128,128]{2,1,0:T(8,128)(2,1)}, u32[]{:S(2)}, u32[]{:S(2)}) async-start(bf16[64,128,128]{2,1,0:T(8,128)(2,1)} %constant_dynamic-update-slice_fusion.64), calls=%async_computation.2 | async-start | bytes 4194304 | tf_op jit(solution)/shard_map/all_to_all | solution.py:33
  655.1 3.8 collective-permute-start.2
  1090.3 107.8 %collective-permute-start.3 = (bf16[128,8192]{1,0:T(8,128)(2,1)S(1)}, bf16[128,8192]{1,0:T(8,128)(2,1)S(1)}, u32[]{:S(2)}, u32[]{:S(2)}) collective-permute-start(bf16[128,8192]{1,0:T(8,128)(2,1)S(1)} %fusion.2), channel_id=1, source_target_pairs={{64,0},{128,64},{192,128},{256,192},{320,256},{384,320},{448,384},... | collective-permute-start | bytes 6291464 | tf_op jit(solution)/shard_map/ppermute | solution.py:15
